TPU v7x, 256 devices: a whole 4x4x8 slice. The times are simulated.
256 devices in a mesh: nodes: 32 (over y, z), feat: 8 (over x, core).
Axes of the slice: x: 4, y: 4, z: 8, core: 2. Of those that a mesh axis runs over, the one named last changes fastest.
Arguments:
- features: bfloat16 [32768, 1024], P('nodes', 'feat'), may hold values from -6 to 6
- ghosts: int32 [1024, 2], P('nodes'), may hold values from 0 to 7, as said below
- slots: int32 [256, 24], P('nodes'), may hold values from 0 to 63
- tile_ids: int32 [256, 24], P('nodes'), may hold values from 0 to 15
- degrees: int32 [256], P('nodes'), may hold values from 1 to 24, 2048 in all
- tile_table: bfloat16 [16, 128, 128], replicated, may hold values from -0.5 to 0.5
- weight_one: bfloat16 [1024, 1024], P(None, 'feat'), may hold values from -0.1875 to 0.1875
- weight_two: bfloat16 [1024, 1024], P(None, 'feat'), may hold values from -0.1875 to 0.1875
- cotangent: bfloat16 [32768, 1024], P('nodes', 'feat'), may hold values from -0.15625 to 0.15625
Outputs:
- output: bfloat16 [32768, 1024], P('nodes', 'feat')
- grad_one: float32 [1024, 1024], P('nodes', 'feat')
- grad_two: float32 [1024, 1024], P('nodes', 'feat')
Inputs may be any that keep to these rules, and one draw needn't show every extreme that they name: `ghosts`: row d * 32 + p holds 2 distinct block indices of device p. The degrees sum to 2048; the largest is 24.
All inputs are finite; a program needn't handle non-finite values. No bound on the sum of `degrees` on one device may be relied on, other than what follows from the above.
Results may differ from a plain program's by a relative error of at most 0.0061.
Values may be sent and summed in bfloat16 or wider, within the bound.
A program may use at most 64 MiB of HBM per device.

v0:
```python
import jax
import jax.numpy as jnp
from jax import lax
from jax.sharding import PartitionSpec as P

entry_step = 8


def entry_weights(degrees, slot_width):
    position = lax.broadcasted_iota(jnp.int32, (degrees.shape[0], slot_width), 1)
    inverse_root = lax.rsqrt(degrees.astype(jnp.float32))[:, None]
    return jnp.where(position < degrees[:, None], inverse_root, 0.0)


def collect(ghost_rows, slots, tile_ids, weights, tile_table, passes):
    block_count = slots.shape[0]
    block_size = ghost_rows.shape[1]
    feat_width = ghost_rows.shape[2]

    def collect_advance(turn_index, running):
        first_entry = turn_index * entry_step
        near_ids = lax.dynamic_slice_in_dim(slots, first_entry, entry_step, 1)
        tile_pick = lax.dynamic_slice_in_dim(tile_ids, first_entry, entry_step, 1)
        entry_share = lax.dynamic_slice_in_dim(weights, first_entry, entry_step, 1)
        near_rows = ghost_rows[near_ids]
        picked = tile_table[tile_pick]
        products = jnp.einsum(
            "bkij,bkjf->bkif", picked, near_rows, preferred_element_type=jnp.float32
        )
        return running + jnp.sum(entry_share[:, :, None, None] * products, axis=1)

    start_value = jnp.zeros((block_count, block_size, feat_width), jnp.float32)
    return lax.fori_loop(0, passes, collect_advance, start_value)


def neighbours(values, requests, slots, tile_ids, weights, tile_table, passes):
    block_count = slots.shape[0]
    block_size = tile_table.shape[1]
    blocks = values.reshape(block_count, block_size, values.shape[1])
    outgoing = blocks[requests]
    arrived = lax.all_to_all(outgoing, "nodes", split_axis=0, concat_axis=0, tiled=True)
    flat_rows = arrived.reshape(-1, block_size, arrived.shape[3])
    running = collect(flat_rows, slots, tile_ids, weights, tile_table, passes)
    return (blocks.astype(jnp.float32) + running).astype(jnp.bfloat16).reshape(values.shape)


def scatter_back(grad_rows, requests, slots, tile_ids, weights, tile_table, passes, peer_count):
    block_count = slots.shape[0]
    block_size = tile_table.shape[1]
    feat_width = grad_rows.shape[1]
    blocks = grad_rows.reshape(block_count, block_size, feat_width)
    slot_total = requests.shape[0] * requests.shape[1]

    def scatter_advance(turn_index, running):
        first_entry = turn_index * entry_step
        near_ids = lax.dynamic_slice_in_dim(slots, first_entry, entry_step, 1)
        tile_pick = lax.dynamic_slice_in_dim(tile_ids, first_entry, entry_step, 1)
        entry_share = lax.dynamic_slice_in_dim(weights, first_entry, entry_step, 1)
        picked = tile_table[tile_pick]
        products = jnp.einsum("bkji,bjf->bkif", picked, blocks, preferred_element_type=jnp.float32)
        scaled = entry_share[:, :, None, None] * products
        return running + jax.ops.segment_sum(
            scaled.reshape(-1, block_size, feat_width),
            near_ids.reshape(-1),
            num_segments=slot_total,
        )

    start_value = jnp.zeros((slot_total, block_size, feat_width), jnp.float32)
    outbound = lax.fori_loop(0, passes, scatter_advance, start_value)
    outgoing = outbound.astype(jnp.bfloat16).reshape(peer_count, -1, block_size, feat_width)
    arrived = lax.all_to_all(outgoing, "nodes", split_axis=0, concat_axis=0, tiled=True)
    flat_rows = arrived.reshape(-1, block_size, arrived.shape[3]).astype(jnp.float32)
    running = jax.ops.segment_sum(flat_rows, requests.reshape(-1), num_segments=block_count)
    return (blocks.astype(jnp.float32) + running).reshape(grad_rows.shape)


def widen(values):
    return lax.all_gather(values, "feat", axis=1, tiled=True)


def weight_grad(wide_rows, local_rows):
    shares = lax.dot_general(
        wide_rows, local_rows, (((0,), (0,)), ((), ())), preferred_element_type=jnp.float32
    )
    peer_count = lax.axis_size("nodes")
    shares = shares.reshape(peer_count, -1, shares.shape[1])
    arrived = lax.all_to_all(shares, "nodes", split_axis=0, concat_axis=0, tiled=True)
    return jnp.sum(arrived, axis=0)


def on_device(
    features, ghosts, slots, tile_ids, degrees, tile_table, weight_one, weight_two, cotangent
):
    peer_count = lax.axis_size("nodes")
    requests = lax.all_to_all(ghosts, "nodes", split_axis=0, concat_axis=0, tiled=True)
    weights = entry_weights(degrees, slots.shape[1])
    passes = slots.shape[1] // entry_step
    agg_one = neighbours(features, requests, slots, tile_ids, weights, tile_table, passes)
    wide_one = widen(agg_one)
    pre_one = jnp.dot(wide_one, weight_one, preferred_element_type=jnp.float32)
    hidden = jax.nn.silu(pre_one).astype(jnp.bfloat16)
    agg_two = neighbours(hidden, requests, slots, tile_ids, weights, tile_table, passes)
    wide_two = widen(agg_two)
    output = jnp.dot(wide_two, weight_two, preferred_element_type=jnp.float32).astype(jnp.bfloat16)
    grad_two = weight_grad(wide_two, cotangent)
    partial_terms = lax.dot_general(
        cotangent, weight_two, (((1,), (1,)), ((), ())), preferred_element_type=jnp.float32
    )
    grad_sum = lax.psum_scatter(partial_terms, "feat", scatter_dimension=1, tiled=True)
    grad_agg = grad_sum.astype(jnp.bfloat16)
    back_hidden = scatter_back(
        grad_agg, requests, slots, tile_ids, weights, tile_table, passes, peer_count
    )
    sigmoid_pre = jax.nn.sigmoid(pre_one)
    back_pre = (back_hidden * sigmoid_pre * (1.0 + pre_one * (1.0 - sigmoid_pre))).astype(
        jnp.bfloat16
    )
    grad_one = weight_grad(wide_one, back_pre)
    return (output, grad_one, grad_two)


def solution(mesh):
    return jax.shard_map(
        on_device,
        mesh=mesh,
        in_specs=(
            P("nodes", "feat"),
            P("nodes", None),
            P("nodes", None),
            P("nodes", None),
            P("nodes"),
            P(),
            P(None, "feat"),
            P(None, "feat"),
            P("nodes", "feat"),
        ),
        out_specs=(P("nodes", "feat"), P("nodes", "feat"), P("nodes", "feat")),
        check_vma=False,
    )
```

profile of v0, /device:TPU:32, one launch (start us, length us, event | category | flops | bytes accessed | tf_op | source)
XLA Modules:
  0.0 351.8 jit_solution(16912315060916707319)
XLA Ops:
  7.2 0.9 copy-done
  8.1 3.6 %fusion.4 = f32[1024,1024]{1,0:T(8,128)} fusion(bf16[1024,128]{1,0:T(8,128)(2,1)S(1)} %copy-done, bf16[1024,128]{1,0:T(8,128)(2,1)} %param.22), kind=kOutput, calls=%fused_computation.43 | convolution fusion | flops 268435456 | bytes 4718592 | tf_op jit(solution)/shard_map/dot_general | solution.py:106
  12.5 19.8 %all_to_all.37 = s32[32,1,2]{2,1,0:T(1,128)S(1)} all-to-all(s32[32,1,2]{2,1,0:T(1,128)S(1)} %copy.19), channel_id=1, replica_groups=mesh['nodes'=32,'feat'=8] {'nodes'}, dimensions={0} | all-to-all | bytes 512 | tf_op jit(solution)/shard_map/all_to_all | solution.py:95
  32.6 2.1 gather_fusion.5
  34.7 5.9 %all-to-all-start.1 = ((bf16[32,2,128,128]{3,2,1,0:T(8,128)(2,1)}), bf16[32,2,128,128]{3,2,1,0:T(8,128)(2,1)}, u32[]{:S(2)}, u32[]{:S(2)}) async-start(bf16[32,2,128,128]{3,2,1,0:T(8,128)(2,1)} %bitcast.7), calls=%async_computation.1 | async-start | bytes 4194304 | tf_op jit(solution)/shard_map/all_to_all | solution.py:41
  40.7 14.4 %reduce-scatter.2.cloned.1.call-done = f32[1024,128]{1,0:T(8,128)} async-done(((f32[1024,1024]{1,0:T(8,128)}), f32[1024,128]{1,0:T(8,128)}) %reduce-scatter.2.cloned.1.call-update) | async-done | bytes 524304 | tf_op jit(solution)/shard_map/reduce_scatter | solution.py:109
  55.1 1.1 convert_element_type.46
  56.2 2.5 broadcast.96
  58.7 53.4 %while.41 = (s32[]{:T(128)}, f32[64,128,128]{2,1,0:T(8,128)}, s32[8,24]{1,0:T(8,128)S(1)}, f32[8,24]{1,0:T(8,128)S(1)}, s32[8,24]{1,0:T(8,128)S(1)}, /*index=5*/...) while((s32[]{:T(128)}, f32[64,128,128]{2,1,0:T(8,128)}, ...), condition=%wide.region_9.10_spmd, body=%wide.region_7.9_spmd.sunk | while | flops 270533824 | bytes 23338668 | solution.py:69
  59.0 1.0 gather_fusion
  60.0 3.0 convolution_multiply_fusion.2
  63.0 13.5 %scatter_fusion = f32[64,128,128]{2,1,0:T(8,128)} fusion(f32[64,128,128]{2,1,0:T(8,128)} %get-tuple-element.629, s32[64]{0:T(128)S(1)} %reshape.238, f32[64,128,128]{2,1,0:T(8,128)} %bitcast.76), kind=kCustom, calls=%fused_computation.7.clone.1 | custom fusion | flops 1048576 | bytes 12583168 | tf_op jit(solution)/shard_map/while/body/eval_jaxpr/scatter-add | solution.py:62
  76.7 1.0 gather_fusion
  77.8 3.0 convolution_multiply_fusion.2
  80.7 13.6 %scatter_fusion = f32[64,128,128]{2,1,0:T(8,128)} fusion(f32[64,128,128]{2,1,0:T(8,128)} %get-tuple-element.629, s32[64]{0:T(128)S(1)} %reshape.238, f32[64,128,128]{2,1,0:T(8,128)} %bitcast.76), kind=kCustom, calls=%fused_computation.7.clone.1 | custom fusion | flops 1048576 | bytes 12583168 | tf_op jit(solution)/shard_map/while/body/eval_jaxpr/scatter-add | solution.py:62
  94.6 1.0 gather_fusion
  95.6 3.0 convolution_multiply_fusion.2
  98.6 13.5 %scatter_fusion = f32[64,128,128]{2,1,0:T(8,128)} fusion(f32[64,128,128]{2,1,0:T(8,128)} %get-tuple-element.629, s32[64]{0:T(128)S(1)} %reshape.238, f32[64,128,128]{2,1,0:T(8,128)} %bitcast.76), kind=kCustom, calls=%fused_computation.7.clone.1 | custom fusion | flops 1048576 | bytes 12583168 | tf_op jit(solution)/shard_map/while/body/eval_jaxpr/scatter-add | solution.py:62
  112.1 3.9 %convert_element_type.48 = bf16[64,128,128]{2,1,0:T(8,128)(2,1)} convert(f32[64,128,128]{2,1,0:T(8,128)} %get-tuple-element.377) | non-fusion elementwise | flops 1048576 | bytes 6291456 | tf_op jit(solution)/shard_map/convert_element_type | solution.py:70
  116.0 10.2 %all-to-all-start.3 = ((bf16[32,2,128,128]{3,2,1,0:T(8,128)(2,1)}), bf16[32,2,128,128]{3,2,1,0:T(8,128)(2,1)}, u32[]{:S(2)}, u32[]{:S(2)}) async-start(bf16[32,2,128,128]{3,2,1,0:T(8,128)(2,1)} %bitcast.15), calls=%async_computation.4 | async-start | bytes 4194304 | tf_op jit(solution)/shard_map/all_to_all | solution.py:71
  126.3 30.5 %while.42 = (s32[]{:T(128)}, f32[8,128,128]{2,1,0:T(8,128)}, f32[8,24]{1,0:T(8,128)S(1)}, s32[8,24]{1,0:T(8,128)S(1)}, bf16[16,128,128]{2,1,0:T(8,128)(2,1)S(1)}...) while((s32[]{:T(128)}, f32[8,128,128]{2,1,0:T(8,128)}, ...), condition=%wide.region_2.3_spmd.clone, body=%wide.region_0.2_spmd.clone.sunk | while | flops 270666112 | bytes 14692277 | solution.py:33
  126.5 1.0 gather_fusion.1
  127.5 3.7 %gather_fusion.2 = bf16[64,128,128]{2,1,0:T(8,128)(2,1)} fusion(bf16[64,128,128]{2,1,0:T(8,128)(2,1)} %get-tuple-element.678, s32[1024]{0:T(1024)S(1)} %pad_clamp_fusion.13), kind=kCustom, calls=%fused_computation.1.clone.clone.1 | custom fusion | bytes 4194560 | tf_op jit(solution)/shard_map/while/body/eval_jaxpr/gather | solution.py:25
  131.3 3.1 multiply_reduce_fusion.4
  134.5 1.9 select_add_fusion.4
  136.6 1.0 gather_fusion.1
  137.6 3.7 %gather_fusion.2 = bf16[64,128,128]{2,1,0:T(8,128)(2,1)} fusion(bf16[64,128,128]{2,1,0:T(8,128)(2,1)} %get-tuple-element.678, s32[1024]{0:T(1024)S(1)} %pad_clamp_fusion.13), kind=kCustom, calls=%fused_computation.1.clone.clone.1 | custom fusion | bytes 4194560 | tf_op jit(solution)/shard_map/while/body/eval_jaxpr/gather | solution.py:25
  141.4 3.1 multiply_reduce_fusion.4
  144.6 2.1 select_add_fusion.4
  146.8 1.0 gather_fusion.1
  147.8 3.7 %gather_fusion.2 = bf16[64,128,128]{2,1,0:T(8,128)(2,1)} fusion(bf16[64,128,128]{2,1,0:T(8,128)(2,1)} %get-tuple-element.678, s32[1024]{0:T(1024)S(1)} %pad_clamp_fusion.13), kind=kCustom, calls=%fused_computation.1.clone.clone.1 | custom fusion | bytes 4194560 | tf_op jit(solution)/shard_map/while/body/eval_jaxpr/gather | solution.py:25
  151.6 3.1 multiply_reduce_fusion.4
  154.8 2.1 select_add_fusion.4
  156.8 1.8 add_convert_fusion.1
  159.2 0.7 reduce.3
  160.0 13.5 %all-to-all-done.3 = bf16[32,2,128,128]{3,2,1,0:T(8,128)(2,1)} async-done(((bf16[32,2,128,128]{3,2,1,0:T(8,128)(2,1)}), bf16[32,2,128,128]{3,2,1,0:T(8,128)(2,1)}, u32[]{:S(2)}, u32[]{:S(2)}) %all-to-all-start.3) | async-done | bytes 2097184 | tf_op jit(solution)/shard_map/all_to_all | solution.py:71
  173.5 4.1 %bitcast_convert_fusion = f32[64,128,128]{2,1,0:T(8,128)} fusion(bf16[32,2,128,128]{3,2,1,0:T(8,128)(2,1)} %all-to-all-done.3), kind=kLoop, calls=%fused_computation.29 | loop fusion | flops 1048576 | bytes 6291456 | tf_op jit(solution)/shard_map/convert_element_type | solution.py:72
  177.6 8.8 %scatter_fusion.1 = f32[8,128,128]{2,1,0:T(8,128)S(1)} fusion(f32[8,128,128]{2,1,0:T(8,128)S(1)} %convert_element_type.47, s32[64]{0:T(128)S(1)} %reshape.170, f32[64,128,128]{2,1,0:T(8,128)} %bitcast_convert_fusion), kind=kCustom, calls=%fused_computation.8 | custom fusion | flops 1048576 | bytes 12583168 | tf_op jit(solution)/shard_map/scatter-add | solution.py:73
  186.4 0.8 all-gather.3.cloned.1.call-done
  187.2 3.0 fusion.2
  190.2 2.1 gather_fusion.6
  192.3 10.1 %all-to-all-start.2 = ((bf16[32,2,128,128]{3,2,1,0:T(8,128)(2,1)}), bf16[32,2,128,128]{3,2,1,0:T(8,128)(2,1)S(1)}, u32[]{:S(2)}, u32[]{:S(2)}) async-start(bf16[32,2,128,128]{3,2,1,0:T(8,128)(2,1)} %bitcast.88), calls=%async_computation.2 | async-start | bytes 4194304 | tf_op jit(solution)/shard_map/all_to_all | solution.py:41
  202.7 49.7 %all-to-all-done.2 = bf16[32,2,128,128]{3,2,1,0:T(8,128)(2,1)S(1)} async-done(((bf16[32,2,128,128]{3,2,1,0:T(8,128)(2,1)}), bf16[32,2,128,128]{3,2,1,0:T(8,128)(2,1)S(1)}, u32[]{:S(2)}, u32[]{:S(2)}) %all-to-all-start.2) | async-done | bytes 2097184 | tf_op jit(solution)/shard_map/all_to_all | solution.py:41
  252.4 31.2 %while.43 = (s32[]{:T(128)}, f32[8,128,128]{2,1,0:T(8,128)}, f32[8,24]{1,0:T(8,128)S(1)}, s32[8,24]{1,0:T(8,128)S(1)}, bf16[16,128,128]{2,1,0:T(8,128)(2,1)S(1)}...) while((s32[]{:T(128)}, f32[8,128,128]{2,1,0:T(8,128)}, ...), condition=%wide.region_5.6_spmd.clone, body=%wide.region_3.5_spmd.clone.sunk | while | flops 270666112 | bytes 14692277 | solution.py:33
  252.5 2.1 gather_fusion.3
  254.8 2.1 gather_fusion.4
  257.0 3.8 %multiply_reduce_fusion.5 = f32[8,128,128]{2,1,0:T(8,128)} fusion(bf16[8,8,128,128]{3,2,1,0:T(8,128)(2,1)} %bitcast.80, bf16[8,8,128,128]{3,2,1,0:T(8,128)(2,1)} %bitcast.82, f32[8,8]{1,0:T(8,128)S(1)} %constant_dynamic-slice_fusion.9), kind=kOutput, calls=%fused_computation.22.clone.1 | convolution fusion | flops 270401536 | bytes 4718848 | tf_op jit(solution)/shard_map/while/body/eval_jaxpr/bkij,bkjf->bkif/dot_general | solution.py:27
  260.8 1.9 select_add_fusion.5
  262.8 2.1 gather_fusion.3
  265.1 2.1 gather_fusion.4
  267.3 3.8 %multiply_reduce_fusion.5 = f32[8,128,128]{2,1,0:T(8,128)} fusion(bf16[8,8,128,128]{3,2,1,0:T(8,128)(2,1)} %bitcast.80, bf16[8,8,128,128]{3,2,1,0:T(8,128)(2,1)} %bitcast.82, f32[8,8]{1,0:T(8,128)S(1)} %constant_dynamic-slice_fusion.9), kind=kOutput, calls=%fused_computation.22.clone.1 | convolution fusion | flops 270401536 | bytes 4718848 | tf_op jit(solution)/shard_map/while/body/eval_jaxpr/bkij,bkjf->bkif/dot_general | solution.py:27
  271.1 2.1 select_add_fusion.5
  273.3 2.1 gather_fusion.3
  275.5 2.1 gather_fusion.4
  277.7 3.8 %multiply_reduce_fusion.5 = f32[8,128,128]{2,1,0:T(8,128)} fusion(bf16[8,8,128,128]{3,2,1,0:T(8,128)(2,1)} %bitcast.80, bf16[8,8,128,128]{3,2,1,0:T(8,128)(2,1)} %bitcast.82, f32[8,8]{1,0:T(8,128)S(1)} %constant_dynamic-slice_fusion.9), kind=kOutput, calls=%fused_computation.22.clone.1 | convolution fusion | flops 270401536 | bytes 4718848 | tf_op jit(solution)/shard_map/while/body/eval_jaxpr/bkij,bkjf->bkif/dot_general | solution.py:27
  281.5 2.1 select_add_fusion.5
  283.6 1.8 add_convert_fusion
  285.4 3.1 fusion.5
  288.5 6.9 %all-to-all-start.4 = ((f32[32,32,128]{2,1,0:T(8,128)}), f32[32,32,128]{2,1,0:T(8,128)S(1)}, u32[]{:S(2)}, u32[]{:S(2)}) async-start(f32[32,32,128]{2,1,0:T(8,128)} %bitcast.18), calls=%async_computation.5 | async-start | bytes 1048576 | tf_op jit(solution)/shard_map/all_to_all | solution.py:87
  295.4 17.7 %all-gather.5.cloned.1.call-done = bf16[1024,1024]{1,0:T(8,128)(2,1)} async-done(((bf16[1024,128]{1,0:T(8,128)(2,1)}), bf16[1024,1024]{1,0:T(8,128)(2,1)}) %all-gather.5.cloned.1.call-update) | async-done | bytes 2097168 | tf_op jit(solution)/shard_map/all_gather | solution.py:78
  313.1 3.3 fusion.6
  316.4 10.1 %all-to-all-start.5 = ((f32[32,32,128]{2,1,0:T(8,128)}), f32[32,32,128]{2,1,0:T(8,128)S(1)}, u32[]{:S(2)}, u32[]{:S(2)}) async-start(f32[32,32,128]{2,1,0:T(8,128)} %bitcast.19), calls=%async_computation.6 | async-start | bytes 1048576 | tf_op jit(solution)/shard_map/all_to_all | solution.py:87
  327.2 2.4 convolution_convert_fusion
  329.5 15.0 %all-to-all-done.5 = f32[32,32,128]{2,1,0:T(8,128)S(1)} async-done(((f32[32,32,128]{2,1,0:T(8,128)}), f32[32,32,128]{2,1,0:T(8,128)S(1)}, u32[]{:S(2)}, u32[]{:S(2)}) %all-to-all-start.5) | async-done | bytes 524320 | tf_op jit(solution)/shard_map/all_to_all | solution.py:87
  (91 shorter events, 6.3 us)
Async XLA Ops:
  7.2 1.0 copy-start
  7.2 47.9 %reduce-scatter.2.cloned.1.call-start = ((), (), s32[]{:S(2)}) async-start(), calls=%async_computation.9 | async-start | bytes 4718592 | tf_op jit(solution)/shard_map/reduce_scatter | solution.py:109
  11.7 0.7 copy-start.6
  11.7 20.8 %copy-start.2 = (bf16[1024,128]{1,0:T(8,128)(2,1)S(1)}, bf16[1024,128]{1,0:T(8,128)(2,1)}, u32[]{:S(2)}) copy-start(bf16[1024,128]{1,0:T(8,128)(2,1)} %param.15) | copy-start | bytes 786436
  34.7 5.9 %copy-start.7 = (s32[8]{0:T(128)S(1)}, s32[8]{0:T(128)}, u32[]{:S(2)}) copy-start(s32[8]{0:T(128)} %param.19) | copy-start | bytes 100
  34.7 81.3 %all-to-all-start.1 = ((bf16[32,2,128,128]{3,2,1,0:T(8,128)(2,1)}), bf16[32,2,128,128]{3,2,1,0:T(8,128)(2,1)}, u32[]{:S(2)}, u32[]{:S(2)}) async-start(bf16[32,2,128,128]{3,2,1,0:T(8,128)(2,1)} %bitcast.7), calls=%async_computation.1 | async-start | bytes 4194304 | tf_op jit(solution)/shard_map/all_to_all | solution.py:41
  56.2 2.5 copy-start.1
  56.2 2.5 copy-start.4
  56.2 2.5 copy-start.5
  116.0 57.5 %all-to-all-start.3 = ((bf16[32,2,128,128]{3,2,1,0:T(8,128)(2,1)}), bf16[32,2,128,128]{3,2,1,0:T(8,128)(2,1)}, u32[]{:S(2)}, u32[]{:S(2)}) async-start(bf16[32,2,128,128]{3,2,1,0:T(8,128)(2,1)} %bitcast.15), calls=%async_computation.4 | async-start | bytes 4194304 | tf_op jit(solution)/shard_map/all_to_all | solution.py:71
  126.3 60.9 %all-gather.3.cloned.1.call-start = ((), (), s32[]{:S(2)}) async-start(), calls=%async_computation.7 | async-start | bytes 2359296 | tf_op jit(solution)/shard_map/all_gather | solution.py:78
  177.6 9.6 %copy-start.8 = (bf16[1024,128]{1,0:T(8,128)(2,1)S(1)}, bf16[1024,128]{1,0:T(8,128)(2,1)}, u32[]{:S(2)}) copy-start(bf16[1024,128]{1,0:T(8,128)(2,1)} %param.21) | copy-start | bytes 786436
  192.3 60.0 %all-to-all-start.2 = ((bf16[32,2,128,128]{3,2,1,0:T(8,128)(2,1)}), bf16[32,2,128,128]{3,2,1,0:T(8,128)(2,1)S(1)}, u32[]{:S(2)}, u32[]{:S(2)}) async-start(bf16[32,2,128,128]{3,2,1,0:T(8,128)(2,1)} %bitcast.88), calls=%async_computation.2 | async-start | bytes 4194304 | tf_op jit(solution)/shard_map/all_to_all | solution.py:41
  202.4 110.7 %all-gather.5.cloned.1.call-start = ((), (), s32[]{:S(2)}) async-start(), calls=%async_computation.8 | async-start | bytes 2359296 | tf_op jit(solution)/shard_map/all_gather | solution.py:78
  288.5 27.9 %all-to-all-start.4 = ((f32[32,32,128]{2,1,0:T(8,128)}), f32[32,32,128]{2,1,0:T(8,128)S(1)}, u32[]{:S(2)}, u32[]{:S(2)}) async-start(f32[32,32,128]{2,1,0:T(8,128)} %bitcast.18), calls=%async_computation.5 | async-start | bytes 1048576 | tf_op jit(solution)/shard_map/all_to_all | solution.py:87
  313.1 14.0 %copy-start.3 = (bf16[1024,1024]{1,0:T(8,128)(2,1)S(1)}, bf16[1024,1024]{1,0:T(8,128)(2,1)}, u32[]{:S(2)}) copy-start(bf16[1024,1024]{1,0:T(8,128)(2,1)} %all-gather.5.cloned.1.call-done) | copy-start | bytes 6291460
  316.4 28.1 %all-to-all-start.5 = ((f32[32,32,128]{2,1,0:T(8,128)}), f32[32,32,128]{2,1,0:T(8,128)S(1)}, u32[]{:S(2)}, u32[]{:S(2)}) async-start(f32[32,32,128]{2,1,0:T(8,128)} %bitcast.19), calls=%async_computation.6 | async-start | bytes 1048576 | tf_op jit(solution)/shard_map/all_to_all | solution.py:87
Sparse Core Ops, SparseCore 0:
  11.9 43.1 reduce-scatter.1
  158.8 28.3 all-gather.2
  285.5 27.5 all-gather.4
where the time goes:
time: 354 us; the launch traced here: 352 us
  waiting for transfers between devices  111 us (31%)
  other arithmetic  77.1 us (22%)
  matrix products  45.1 us (13%)
  starting transfers between devices  43.4 us (12%)
  local copies, waits for them, and re-layouts  41.2 us (12%)
  blocking collectives  19.8 us (6%)
  between operations  13.9 us (4%)
    all_to_all x2, waiting for transfers between devices, neighbours(): lax.all_to_all(outgoing, 'nodes', split_axis=0, concat_axis=0, tiled=True)  49.7 us
    scatter-add x3, other arithmetic, scatter_advance(): jax.ops.segment_sum(scaled.reshape(-1, block_size, feat_width), near_ids....  40.7 us
    dot_general x6, matrix products, collect_advance(): jnp.einsum('bkij,bkjf->bkif', picked, near_rows, preferred_element_type=j...  20.8 us
    all_to_all x1, blocking collectives, on_device(): lax.all_to_all(ghosts, 'nodes', split_axis=0, concat_axis=0, tiled=True)  19.8 us
    all_gather x2, waiting for transfers between devices, widen(): return lax.all_gather(values, 'feat', axis=1, tiled=True)  18.5 us
    gather x6, local copies, waits for them, and re-layouts, collect_advance(): near_rows = ghost_rows[near_ids]  17.6 us
    all_to_all x2, starting transfers between devices, weight_grad(): lax.all_to_all(shares, 'nodes', split_axis=0, concat_axis=0, tiled=True)  17 us
    all_to_all x2, starting transfers between devices, neighbours(): lax.all_to_all(outgoing, 'nodes', split_axis=0, concat_axis=0, tiled=True)  16 us
  transfers between devices with their start and end apart: 8, of which 6 were waited for; matrix products, arithmetic and copies ran while one was open for 34% of the time, Pallas kernels for 0%

commit v1 on v0

--- a/solution.py
+++ b/solution.py
@@ -75,7 +75,9 @@
 
 
 def widen(values):
-    return lax.all_gather(values, "feat", axis=1, tiled=True)
+    return jnp.concatenate(
+        lax.all_to_all(jnp.stack([values] * lax.axis_size("feat")), "feat", 0, 0), axis=1
+    )
 
 
 def weight_grad(wide_rows, local_rows):

time: 354 us -> 388 us (1.096)
  waiting for transfers between devices: 111 us -> 146 us
    all_to_all x0 -> x2, waiting for transfers between devices: none -> 37 us  [widen(): lax.all_to_all(jnp.stack([values] * lax.axis_size('feat')), 'feat', 0, 0)]
    all_gather x2 -> x0, waiting for transfers between devices: 18.5 us -> none  [widen(): return lax.all_gather(values, 'feat', axis=1, tiled=True)]
    all_to_all x2, waiting for transfers between devices: 15 us -> 29.8 us  [weight_grad(): lax.all_to_all(shares, 'nodes', split_axis=0, concat_axis=0, tiled=True)]
    all_to_all x0 -> x2, starting transfers between devices: none -> 8.08 us  [widen(): lax.all_to_all(jnp.stack([values] * lax.axis_size('feat')), 'feat', 0, 0)]
    all_to_all x2, starting transfers between devices: 17 us -> 12 us  [weight_grad(): lax.all_to_all(shares, 'nodes', split_axis=0, concat_axis=0, tiled=True)]
  transfers between devices with their start and end apart: 8 -> 8, of which waited for: 6 -> 7; matrix products, arithmetic and copies ran while one was open for 34% -> 30% of each run, Pallas kernels for 0% -> 0%
where the time goes in v1:
time: 388 us; the launch traced here: 386 us
  waiting for transfers between devices  146 us (38%)
  other arithmetic  75.6 us (19%)
  local copies, waits for them, and re-layouts  44.8 us (12%)
  matrix products  43.4 us (11%)
  starting transfers between devices  42.7 us (11%)
  blocking collectives  19.8 us (5%)
  between operations  14.2 us (4%)
    all_to_all x2, waiting for transfers between devices, neighbours(): lax.all_to_all(outgoing, 'nodes', split_axis=0, concat_axis=0, tiled=True)  48.8 us
    scatter-add x3, other arithmetic, scatter_advance(): jax.ops.segment_sum(scaled.reshape(-1, block_size, feat_width), near_ids....  40.6 us
    all_to_all x2, waiting for transfers between devices, widen(): lax.all_to_all(jnp.stack([values] * lax.axis_size('feat')), 'feat', 0, 0)  37 us
    all_to_all x2, waiting for transfers between devices, weight_grad(): lax.all_to_all(shares, 'nodes', split_axis=0, concat_axis=0, tiled=True)  29.8 us
    dot_general x6, matrix products, collect_advance(): jnp.einsum('bkij,bkjf->bkif', picked, near_rows, preferred_element_type=j...  20.8 us
    all_to_all x1, blocking collectives, on_device(): lax.all_to_all(ghosts, 'nodes', split_axis=0, concat_axis=0, tiled=True)  19.8 us
    gather x6, local copies, waits for them, and re-layouts, collect_advance(): near_rows = ghost_rows[near_ids]  17.6 us
    all_to_all x1, waiting for transfers between devices, scatter_back(): lax.all_to_all(outgoing, 'nodes', split_axis=0, concat_axis=0, tiled=True)  15.5 us
  transfers between devices with their start and end apart: 8, of which 7 were waited for; matrix products, arithmetic and copies ran while one was open for 30% of the time, Pallas kernels for 0%

profile of v1, /device:TPU:32, one launch (start us, length us, event | category | flops | bytes accessed | tf_op | source)
XLA Modules:
  0.0 386.1 jit_solution(11458445460223196493)
XLA Ops:
  8.1 3.6 fusion.8
  12.5 19.8 %all_to_all.47 = s32[32,1,2]{2,1,0:T(1,128)S(1)} all-to-all(s32[32,1,2]{2,1,0:T(1,128)S(1)} %copy.23), channel_id=1, replica_groups=mesh['nodes'=32,'feat'=8] {'nodes'}, dimensions={0} | all-to-all | bytes 512 | tf_op jit(solution)/shard_map/all_to_all | solution.py:97
  32.6 2.2 gather_fusion.5
  34.7 5.9 %all-to-all-start.1 = ((bf16[32,2,128,128]{3,2,1,0:T(8,128)(2,1)}), bf16[32,2,128,128]{3,2,1,0:T(8,128)(2,1)}, u32[]{:S(2)}, u32[]{:S(2)}) async-start(bf16[32,2,128,128]{3,2,1,0:T(8,128)(2,1)} %bitcast.7), calls=%async_computation.1 | async-start | bytes 4194304 | tf_op jit(solution)/shard_map/all_to_all | solution.py:41
  40.7 14.4 %reduce-scatter.2.cloned.1.call-done = f32[1024,128]{1,0:T(8,128)} async-done(((f32[1024,1024]{1,0:T(8,128)}), f32[1024,128]{1,0:T(8,128)}) %reduce-scatter.2.cloned.1.call-update) | async-done | bytes 524304 | tf_op jit(solution)/shard_map/reduce_scatter | solution.py:111
  55.1 1.1 convert_element_type.46
  56.2 2.5 broadcast.98
  58.7 53.4 %while.41 = (s32[]{:T(128)}, f32[64,128,128]{2,1,0:T(8,128)}, s32[8,24]{1,0:T(8,128)S(1)}, f32[8,24]{1,0:T(8,128)S(1)}, s32[8,24]{1,0:T(8,128)S(1)}, /*index=5*/...) while((s32[]{:T(128)}, f32[64,128,128]{2,1,0:T(8,128)}, ...), condition=%wide.region_9.10_spmd, body=%wide.region_7.9_spmd.sunk | while | flops 270533824 | bytes 23338668 | solution.py:69
  59.0 1.0 gather_fusion
  60.0 3.0 convolution_multiply_fusion.2
  63.0 13.5 %scatter_fusion = f32[64,128,128]{2,1,0:T(8,128)} fusion(f32[64,128,128]{2,1,0:T(8,128)} %get-tuple-element.629, s32[64]{0:T(128)S(1)} %reshape.248, f32[64,128,128]{2,1,0:T(8,128)} %bitcast.92), kind=kCustom, calls=%fused_computation.7.clone.1 | custom fusion | flops 1048576 | bytes 12583168 | tf_op jit(solution)/shard_map/while/body/eval_jaxpr/scatter-add | solution.py:62
  76.7 1.0 gather_fusion
  77.8 3.0 convolution_multiply_fusion.2
  80.7 13.6 %scatter_fusion = f32[64,128,128]{2,1,0:T(8,128)} fusion(f32[64,128,128]{2,1,0:T(8,128)} %get-tuple-element.629, s32[64]{0:T(128)S(1)} %reshape.248, f32[64,128,128]{2,1,0:T(8,128)} %bitcast.92), kind=kCustom, calls=%fused_computation.7.clone.1 | custom fusion | flops 1048576 | bytes 12583168 | tf_op jit(solution)/shard_map/while/body/eval_jaxpr/scatter-add | solution.py:62
  94.6 1.0 gather_fusion
  95.6 3.0 convolution_multiply_fusion.2
  98.6 13.5 %scatter_fusion = f32[64,128,128]{2,1,0:T(8,128)} fusion(f32[64,128,128]{2,1,0:T(8,128)} %get-tuple-element.629, s32[64]{0:T(128)S(1)} %reshape.248, f32[64,128,128]{2,1,0:T(8,128)} %bitcast.92), kind=kCustom, calls=%fused_computation.7.clone.1 | custom fusion | flops 1048576 | bytes 12583168 | tf_op jit(solution)/shard_map/while/body/eval_jaxpr/scatter-add | solution.py:62
  112.1 3.9 %convert_element_type.48 = bf16[64,128,128]{2,1,0:T(8,128)(2,1)} convert(f32[64,128,128]{2,1,0:T(8,128)} %get-tuple-element.377) | non-fusion elementwise | flops 1048576 | bytes 6291456 | tf_op jit(solution)/shard_map/convert_element_type | solution.py:70
  116.0 10.1 %all-to-all-start.5 = ((bf16[32,2,128,128]{3,2,1,0:T(8,128)(2,1)}), bf16[32,2,128,128]{3,2,1,0:T(8,128)(2,1)}, u32[]{:S(2)}, u32[]{:S(2)}) async-start(bf16[32,2,128,128]{3,2,1,0:T(8,128)(2,1)} %bitcast.22), calls=%async_computation.6 | async-start | bytes 4194304 | tf_op jit(solution)/shard_map/all_to_all | solution.py:71
  126.1 30.5 %while.42 = (s32[]{:T(128)}, f32[8,128,128]{2,1,0:T(8,128)}, f32[8,24]{1,0:T(8,128)S(1)}, s32[8,24]{1,0:T(8,128)S(1)}, bf16[16,128,128]{2,1,0:T(8,128)(2,1)S(1)}...) while((s32[]{:T(128)}, f32[8,128,128]{2,1,0:T(8,128)}, ...), condition=%wide.region_2.3_spmd.clone, body=%wide.region_0.2_spmd.clone.sunk | while | flops 270666112 | bytes 14692277 | solution.py:33
  127.4 3.7 gather_fusion.2
  131.2 3.1 multiply_reduce_fusion.4
  134.3 1.9 select_add_fusion.4
  137.4 3.7 gather_fusion.2
  141.2 3.1 multiply_reduce_fusion.4
  144.4 2.1 select_add_fusion.4
  147.6 3.7 gather_fusion.2
  151.4 3.1 multiply_reduce_fusion.4
  154.6 2.1 select_add_fusion.4
  156.6 1.1 add_convert_fusion.1
  157.9 15.5 %all-to-all-done.5 = bf16[32,2,128,128]{3,2,1,0:T(8,128)(2,1)} async-done(((bf16[32,2,128,128]{3,2,1,0:T(8,128)(2,1)}), bf16[32,2,128,128]{3,2,1,0:T(8,128)(2,1)}, u32[]{:S(2)}, u32[]{:S(2)}) %all-to-all-start.5) | async-done | bytes 2097184 | tf_op jit(solution)/shard_map/all_to_all | solution.py:71
  173.3 1.6 stack.6
  175.0 4.3 %all-to-all-start.2 = ((bf16[8,1024,128]{1,2,0:T(8,128)(2,1)}), bf16[8,1024,128]{1,2,0:T(8,128)(2,1)}, u32[]{:S(2)}, u32[]{:S(2)}) async-start(bf16[8,1024,128]{1,2,0:T(8,128)(2,1)} %stack.6), calls=%async_computation.2 | async-start | bytes 4194304 | tf_op jit(solution)/shard_map/all_to_all | solution.py:79
  180.7 4.1 %bitcast_convert_fusion = f32[64,128,128]{2,1,0:T(8,128)} fusion(bf16[32,2,128,128]{3,2,1,0:T(8,128)(2,1)} %all-to-all-done.5), kind=kLoop, calls=%fused_computation.29 | loop fusion | flops 1048576 | bytes 6291456 | tf_op jit(solution)/shard_map/convert_element_type | solution.py:72
  184.7 8.8 %scatter_fusion.1 = f32[8,128,128]{2,1,0:T(8,128)S(1)} fusion(f32[8,128,128]{2,1,0:T(8,128)S(1)} %convert_element_type.47, s32[64]{0:T(128)S(1)} %reshape.178, f32[64,128,128]{2,1,0:T(8,128)} %bitcast_convert_fusion), kind=kCustom, calls=%fused_computation.8 | custom fusion | flops 1048576 | bytes 12583168 | tf_op jit(solution)/shard_map/scatter-add | solution.py:73
  193.5 13.0 %all-to-all-done.2 = bf16[8,1024,128]{1,2,0:T(8,128)(2,1)} async-done(((bf16[8,1024,128]{1,2,0:T(8,128)(2,1)}), bf16[8,1024,128]{1,2,0:T(8,128)(2,1)}, u32[]{:S(2)}, u32[]{:S(2)}) %all-to-all-start.2) | async-done | bytes 2097184 | tf_op jit(solution)/shard_map/all_to_all | solution.py:79
  206.5 3.1 fusion.2
  209.6 2.2 gather_fusion.6
  211.8 6.6 %all-to-all-start.3 = ((bf16[32,2,128,128]{3,2,1,0:T(8,128)(2,1)}), bf16[32,2,128,128]{3,2,1,0:T(8,128)(2,1)S(1)}, u32[]{:S(2)}, u32[]{:S(2)}) async-start(bf16[32,2,128,128]{3,2,1,0:T(8,128)(2,1)} %bitcast.106), calls=%async_computation.3 | async-start | bytes 4194304 | tf_op jit(solution)/shard_map/all_to_all | solution.py:41
  218.4 48.8 %all-to-all-done.3 = bf16[32,2,128,128]{3,2,1,0:T(8,128)(2,1)S(1)} async-done(((bf16[32,2,128,128]{3,2,1,0:T(8,128)(2,1)}), bf16[32,2,128,128]{3,2,1,0:T(8,128)(2,1)S(1)}, u32[]{:S(2)}, u32[]{:S(2)}) %all-to-all-start.3) | async-done | bytes 2097184 | tf_op jit(solution)/shard_map/all_to_all | solution.py:41
  267.3 31.2 %while.43 = (s32[]{:T(128)}, f32[8,128,128]{2,1,0:T(8,128)}, f32[8,24]{1,0:T(8,128)S(1)}, s32[8,24]{1,0:T(8,128)S(1)}, bf16[16,128,128]{2,1,0:T(8,128)(2,1)S(1)}...) while((s32[]{:T(128)}, f32[8,128,128]{2,1,0:T(8,128)}, ...), condition=%wide.region_5.6_spmd.clone, body=%wide.region_3.5_spmd.clone.sunk | while | flops 270666112 | bytes 14692277 | solution.py:33
  267.4 2.2 gather_fusion.3
  269.7 2.1 gather_fusion.4
  271.9 3.8 multiply_reduce_fusion.5
  275.7 1.9 select_add_fusion.5
  277.7 2.2 gather_fusion.3
  280.0 2.1 gather_fusion.4
  282.2 3.8 multiply_reduce_fusion.5
  286.0 2.1 select_add_fusion.5
  288.2 2.2 gather_fusion.3
  290.5 2.1 gather_fusion.4
  292.7 3.8 multiply_reduce_fusion.5
  296.5 2.1 select_add_fusion.5
  298.5 1.1 add_convert_fusion
  299.8 1.6 stack.7
  301.4 3.7 all-to-all-start.4
  305.1 3.1 fusion.5
  308.2 24.0 %all-to-all-done.4 = bf16[8,1024,128]{1,2,0:T(8,128)(2,1)S(1)} async-done(((bf16[8,1024,128]{1,2,0:T(8,128)(2,1)}), bf16[8,1024,128]{1,2,0:T(8,128)(2,1)S(1)}, u32[]{:S(2)}, u32[]{:S(2)}) %all-to-all-start.4) | async-done | bytes 2097184 | tf_op jit(solution)/shard_map/all_to_all | solution.py:79
  332.2 7.1 %all-to-all-start.6 = ((f32[32,32,128]{2,1,0:T(8,128)}), f32[32,32,128]{2,1,0:T(8,128)S(1)}, u32[]{:S(2)}, u32[]{:S(2)}) async-start(f32[32,32,128]{2,1,0:T(8,128)} %fusion.5), calls=%async_computation.7 | async-start | bytes 1048576 | tf_op jit(solution)/shard_map/all_to_all | solution.py:89
  339.4 1.5 fusion.3
  340.9 15.9 %all-to-all-done.6 = f32[32,32,128]{2,1,0:T(8,128)S(1)} async-done(((f32[32,32,128]{2,1,0:T(8,128)}), f32[32,32,128]{2,1,0:T(8,128)S(1)}, u32[]{:S(2)}, u32[]{:S(2)}) %all-to-all-start.6) | async-done | bytes 524320 | tf_op jit(solution)/shard_map/all_to_all | solution.py:89
  356.8 4.8 %all-to-all-start.7 = ((f32[32,32,128]{2,1,0:T(8,128)}), f32[32,32,128]{2,1,0:T(8,128)S(1)}, u32[]{:S(2)}, u32[]{:S(2)}) async-start(f32[32,32,128]{2,1,0:T(8,128)} %fusion.3), calls=%async_computation.8 | async-start | bytes 1048576 | tf_op jit(solution)/shard_map/all_to_all | solution.py:89
  362.3 2.4 convolution_convert_fusion
  364.7 13.9 %all-to-all-done.7 = f32[32,32,128]{2,1,0:T(8,128)S(1)} async-done(((f32[32,32,128]{2,1,0:T(8,128)}), f32[32,32,128]{2,1,0:T(8,128)S(1)}, u32[]{:S(2)}, u32[]{:S(2)}) %all-to-all-start.7) | async-done | bytes 524320 | tf_op jit(solution)/shard_map/all_to_all | solution.py:89
  (93 shorter events, 10.8 us)
Async XLA Ops:
  7.2 1.0 copy-start
  7.2 47.9 %reduce-scatter.2.cloned.1.call-start = ((), (), s32[]{:S(2)}) async-start(), calls=%async_computation.9 | async-start | bytes 4718592 | tf_op jit(solution)/shard_map/reduce_scatter | solution.py:111
  11.7 0.7 copy-start.6
  11.7 20.8 %copy-start.2 = (bf16[1024,128]{1,0:T(8,128)(2,1)S(1)}, bf16[1024,128]{1,0:T(8,128)(2,1)}, u32[]{:S(2)}) copy-start(bf16[1024,128]{1,0:T(8,128)(2,1)} %param.15) | copy-start | bytes 786436
  34.7 5.9 %copy-start.7 = (s32[8]{0:T(128)S(1)}, s32[8]{0:T(128)}, u32[]{:S(2)}) copy-start(s32[8]{0:T(128)} %param.19) | copy-start | bytes 100
  34.7 81.3 %all-to-all-start.1 = ((bf16[32,2,128,128]{3,2,1,0:T(8,128)(2,1)}), bf16[32,2,128,128]{3,2,1,0:T(8,128)(2,1)}, u32[]{:S(2)}, u32[]{:S(2)}) async-start(bf16[32,2,128,128]{3,2,1,0:T(8,128)(2,1)} %bitcast.7), calls=%async_computation.1 | async-start | bytes 4194304 | tf_op jit(solution)/shard_map/all_to_all | solution.py:41
  56.2 2.5 copy-start.1
  56.2 2.5 copy-start.3
  56.2 2.5 copy-start.4
  116.0 57.3 %all-to-all-start.5 = ((bf16[32,2,128,128]{3,2,1,0:T(8,128)(2,1)}), bf16[32,2,128,128]{3,2,1,0:T(8,128)(2,1)}, u32[]{:S(2)}, u32[]{:S(2)}) async-start(bf16[32,2,128,128]{3,2,1,0:T(8,128)(2,1)} %bitcast.22), calls=%async_computation.6 | async-start | bytes 4194304 | tf_op jit(solution)/shard_map/all_to_all | solution.py:71
  175.0 31.5 %all-to-all-start.2 = ((bf16[8,1024,128]{1,2,0:T(8,128)(2,1)}), bf16[8,1024,128]{1,2,0:T(8,128)(2,1)}, u32[]{:S(2)}, u32[]{:S(2)}) async-start(bf16[8,1024,128]{1,2,0:T(8,128)(2,1)} %stack.6), calls=%async_computation.2 | async-start | bytes 4194304 | tf_op jit(solution)/shard_map/all_to_all | solution.py:79
  184.7 21.8 %copy-start.8 = (bf16[1024,128]{1,0:T(8,128)(2,1)S(1)}, bf16[1024,128]{1,0:T(8,128)(2,1)}, u32[]{:S(2)}) copy-start(bf16[1024,128]{1,0:T(8,128)(2,1)} %param.21) | copy-start | bytes 786436
  211.8 55.5 %all-to-all-start.3 = ((bf16[32,2,128,128]{3,2,1,0:T(8,128)(2,1)}), bf16[32,2,128,128]{3,2,1,0:T(8,128)(2,1)S(1)}, u32[]{:S(2)}, u32[]{:S(2)}) async-start(bf16[32,2,128,128]{3,2,1,0:T(8,128)(2,1)} %bitcast.106), calls=%async_computation.3 | async-start | bytes 4194304 | tf_op jit(solution)/shard_map/all_to_all | solution.py:41
  301.4 3.7 copy-start.5
  301.4 30.9 %all-to-all-start.4 = ((bf16[8,1024,128]{1,2,0:T(8,128)(2,1)}), bf16[8,1024,128]{1,2,0:T(8,128)(2,1)S(1)}, u32[]{:S(2)}, u32[]{:S(2)}) async-start(bf16[8,1024,128]{1,2,0:T(8,128)(2,1)} %stack.7), calls=%async_computation.4 | async-start | bytes 4194304 | tf_op jit(solution)/shard_map/all_to_all | solution.py:79
  332.2 24.6 %all-to-all-start.6 = ((f32[32,32,128]{2,1,0:T(8,128)}), f32[32,32,128]{2,1,0:T(8,128)S(1)}, u32[]{:S(2)}, u32[]{:S(2)}) async-start(f32[32,32,128]{2,1,0:T(8,128)} %fusion.5), calls=%async_computation.7 | async-start | bytes 1048576 | tf_op jit(solution)/shard_map/all_to_all | solution.py:89
  356.8 21.8 %all-to-all-start.7 = ((f32[32,32,128]{2,1,0:T(8,128)}), f32[32,32,128]{2,1,0:T(8,128)S(1)}, u32[]{:S(2)}, u32[]{:S(2)}) async-start(f32[32,32,128]{2,1,0:T(8,128)} %fusion.3), calls=%async_computation.8 | async-start | bytes 1048576 | tf_op jit(solution)/shard_map/all_to_all | solution.py:89
Sparse Core Ops, SparseCore 0:
  11.9 43.1 reduce-scatter.1
